TPU v7x, 512 devices: a whole 4x8x8 slice. The times are simulated.
512 devices in a mesh: seq: 128 (over z_hi, y, x, core), chan: 4 (over z_lo).
Axes of the slice: x: 4, y: 8, z: 8 (z_hi: 2, z_lo: 4; z = z_hi * 4 + z_lo), core: 2. Of those that a mesh axis runs over, the one named last changes fastest.
Arguments:
- residual: bfloat16 [16384, 8192], P('seq', 'chan'), may hold values from -64 to 64
- query_in: bfloat16 [16384, 8192], P('seq', 'chan'), may hold values from -6 to 6
- key_in: bfloat16 [16384, 8192], P('seq', 'chan'), may hold values from -6 to 6
- value_in: bfloat16 [16384, 8192], P('seq', 'chan'), may hold values from -6 to 6
- short_filter: float32 [3, 3, 8192], P(None, None, 'chan'), may hold values from -3.5 to 3.5
- decay_rate: float32 [16, 8192], P(None, 'chan'), may hold values from 0 to 1
- residue: float32 [16, 8192], P(None, 'chan'), may hold values from -1.5 to 1.5
- skip_gain: float32 [8192], P('chan'), may hold values from -3 to 3
- norm_gain: float32 [8192], P('chan'), may hold values from 0.1 to 1.9
Outputs:
- residual_out: bfloat16 [16384, 8192], P('seq', 'chan')
- normed: bfloat16 [16384, 8192], P('seq', 'chan')
All inputs are finite; a program needn't handle non-finite values.
Results may differ from a plain program's by a relative error of at most 0.0055.
Values may be sent and summed in bfloat16 or wider, within the bound.
No kernel may reach another device: no remote copies, remote signals or barrier semaphores. Data moves between devices by JAX's collectives and lax.ppermute only.
A program may use at most 128 MiB of HBM per device.

v0:
```python
import jax
import jax.numpy as jnp
from jax import lax
from jax.sharding import PartitionSpec as P

D = 8192
sub_block = 16
epsilon = 1e-06
highest = lax.Precision.HIGHEST


def shifted(block, axis, distance):
    devices = range(lax.axis_size(axis))
    route = [(i - distance, i) for i in devices if i - distance in devices]
    return lax.ppermute(block, axis, route)


def short_features(inputs, before, tap_weights):
    lag_rows = before.shape[0]
    token_rows = inputs.shape[0]
    extended = jnp.concatenate([before, inputs], axis=0).astype(jnp.float32)
    result = tap_weights[0][None, :] * extended[lag_rows : lag_rows + token_rows]
    for offset in range(1, lag_rows + 1):
        result = (
            result
            + tap_weights[offset][None, :]
            * extended[lag_rows - offset : lag_rows - offset + token_rows]
        )
    return result


def link_states(earlier, later):
    return (earlier[0] * later[0], later[0] * earlier[1] + later[1])


def body(
    residual, query_in, key_in, value_in, short_filter, decay_rate, residue, skip_gain, norm_gain
):
    token_rows, chan_width = residual.shape
    lag_rows = short_filter.shape[1] - 1
    tail_rows = (
        query_in[token_rows - lag_rows :],
        key_in[token_rows - lag_rows :],
        value_in[token_rows - lag_rows :],
    )
    before = shifted((tail_rows[0], tail_rows[1], tail_rows[2]), "seq", 1)
    query_side = short_features(query_in, before[0], short_filter[0])
    key_side = short_features(key_in, before[1], short_filter[1])
    value_side = short_features(value_in, before[2], short_filter[2])
    mixed = key_side * value_side
    weights = residue * jnp.sqrt(2.0 * decay_rate)
    sub_count = token_rows // sub_block
    positions = jnp.arange(sub_block, dtype=jnp.float32)
    local_taps = jnp.sum(
        weights[None] * jnp.exp(-decay_rate[None] * positions[:, None, None]), axis=1
    )
    lag_table = positions[:, None] - positions[None, :]
    one_hot = (lag_table[:, :, None] == positions[None, None, :]).astype(jnp.float32)
    toeplitz = jnp.dot(
        one_hot.reshape(sub_block * sub_block, sub_block), local_taps, precision=highest
    ).reshape(sub_block, sub_block, chan_width)
    blocks = mixed.reshape(sub_count, sub_block, chan_width)
    inside = jnp.sum(toeplitz[None, :, :, :] * blocks[:, None, :, :], axis=2)
    tail_decay = jnp.exp(-decay_rate[None] * (sub_block - 1.0 - positions)[:, None, None])
    sub_states = jnp.sum(blocks[:, :, None, :] * tail_decay[None], axis=1)
    step_decay = jnp.broadcast_to(jnp.exp(-decay_rate * sub_block)[None], sub_states.shape)
    _, running = lax.associative_scan(link_states, (step_decay, sub_states), axis=0)
    block_state = running[sub_count - 1]
    entering = jnp.concatenate([jnp.zeros_like(running[:1]), running[:-1]], axis=0)
    position = lax.axis_index("seq")
    piece = lax.all_gather(
        block_state[None].astype(jnp.bfloat16), "seq", axis=0, tiled=True
    ).astype(jnp.float32)
    members = piece.shape[0]
    sources = jnp.arange(members, dtype=jnp.int32)
    distance = position - 1 - sources
    spans = (token_rows * jnp.maximum(distance, 0)).astype(jnp.float32)
    factors = jnp.exp(-decay_rate[None] * spans[:, None, None])
    masked = jnp.where((distance >= 0)[:, None, None], factors * piece, 0.0)
    carried = jnp.zeros_like(block_state) + jnp.sum(masked, axis=0)
    sub_starts = jnp.arange(sub_count, dtype=jnp.float32) * sub_block
    entering = entering + jnp.exp(-decay_rate[None] * sub_starts[:, None, None]) * carried[None]
    readout = weights[None] * jnp.exp(-decay_rate[None] * (positions + 1.0)[:, None, None])
    across = jnp.sum(readout[None, :, :, :] * entering[:, None, :, :], axis=2)
    convolved = (inside + across).reshape(token_rows, chan_width)
    gated = query_side * (convolved + skip_gain[None, :] * mixed)
    summed = (residual.astype(jnp.float32) + gated).astype(jnp.bfloat16)
    widened = lax.optimization_barrier(summed).astype(jnp.float32)
    row_squares = lax.psum(jnp.sum(widened * widened, axis=1), "chan")
    inverse_rms = lax.rsqrt(row_squares / D + epsilon)
    normed = (widened * inverse_rms[:, None] * norm_gain[None, :]).astype(jnp.bfloat16)
    return (summed, normed)


def solution(mesh):
    in_specs = (
        P("seq", "chan"),
        P("seq", "chan"),
        P("seq", "chan"),
        P("seq", "chan"),
        P(None, None, "chan"),
        P(None, "chan"),
        P(None, "chan"),
        P("chan"),
        P("chan"),
    )
    out_specs = (P("seq", "chan"), P("seq", "chan"))
    return jax.shard_map(body, mesh=mesh, in_specs=in_specs, out_specs=out_specs, check_vma=False)
```

profile of v0, /device:TPU:2, one launch (start us, length us, event | category | flops | bytes accessed | tf_op | source)
XLA Modules:
  0.0 229.2 jit_solution(10560586186307022351)
XLA Ops:
  7.2 0.0 all-gather.2.cloned.1.call-start
  7.2 0.8 slice.156
  8.0 1.9 collective-permute-start.1
  9.9 0.8 slice.163
  10.7 3.5 %collective-permute-start.2 = (bf16[2,2048]{1,0:T(2,128)(2,1)S(1)}, bf16[2,2048]{1,0:T(2,128)(2,1)S(1)}, u32[]{:S(2)}, u32[]{:S(2)}) collective-permute-start(bf16[2,2048]{1,0:T(2,128)(2,1)S(1)} %slice.163), channel_id=1, source_target_pairs={{0,4},{4,8},{8,12},{12,16},{16,20},{20,24},{24,28},{28,32},{32,36}... | collective-permute-start | bytes 24584 | tf_op jit(solution)/shard_map/ppermute | solution.py:15
  14.2 1.0 fusion.24
  15.2 1.0 fusion.21
  16.3 2.4 %exponential_multiply_fusion = (f32[16,16,2048]{2,1,0:T(8,128)}, f32[16,2048]{1,0:T(8,128)S(1)}, f32[16,16,2048]{2,1,0:T(8,128)S(1)}) fusion(f32[16]{0:T(128)S(1)} %get-tuple-element.25, f32[16,2048]{1,0:T(8,128)S(1)} %get-tuple-element.13, f32[16,2048]{1,0:T(8,128)S(1)} %get-tuple-element.14, f32[16]{0:T(128)S(1)} %get-tuple-element.24), kind=kLoop, calls=%fused_computation.5 | loop fusion | flops 3112960 | bytes 4587648 | tf_op jit(solution)/shard_map/mul | solution.py:83
  18.7 1.0 fusion.17
  19.7 0.0 collective-permute-done.1
  19.7 0.1 maximum_convert_fusion.1
  19.9 0.0 collective-permute-done.2
  19.9 0.1 maximum_convert_fusion.2
  20.1 0.7 fusion.4
  20.7 5.8 %multiply_reduce_fusion.1 = (f32[8,16,2048]{2,1,0:T(8,128)S(1)}, f32[8,16,2048]{2,1,0:T(8,128)}) fusion(f32[16,16,2048]{2,1,0:T(8,128)S(1)} %get-tuple-element.10, f32[8,16,2048]{2,1,0:T(8,128)S(1)} %bitcast.23, f32[16,16,2048]{2,1,0:T(8,128)S(1)} %fusion.17), kind=kLoop, calls=%fused_computation.2 | loop fusion | flops 16252928 | bytes 7340032 | tf_op jit(solution)/shard_map/reduce_sum | solution.py:65
  26.5 0.1 slice_add_fusion.1
  26.6 0.8 copy-done.6
  27.6 0.1 pad.23
  27.6 1.5 pad.22
  29.1 1.1 add.100
  30.2 2.3 %pad.62 = f32[7,16,2048]{2,1,0:T(8,128)} pad(f32[4,16,2048]{2,1,0:T(8,128)S(1)} %add.100, f32[]{:T(128)} %constant.13.clone.1), padding=0_0_1x0_0_0x0_0_0 | pad | bytes 1441796
  32.5 1.5 add_convert_fusion
  34.1 0.0 all-gather.2.cloned.1.call-update
  34.1 0.8 slice.149
  34.9 2.1 collective-permute-start
  37.1 1.1 fusion.13
  38.2 2.4 %pad.25 = f32[8,16,2048]{2,1,0:T(8,128)} pad(f32[4,16,2048]{2,1,0:T(8,128)S(1)} %add.100, f32[]{:T(128)} %constant.13.clone.1), padding=1_0_1x0_0_0x0_0_0 | pad | bytes 1572868 | tf_op jit(solution)/shard_map/pad | solution.py:67
  40.5 2.4 %pad.24 = f32[8,16,2048]{2,1,0:T(8,128)} pad(f32[4,16,2048]{2,1,0:T(8,128)S(1)} %pad_maximum_fusion, f32[]{:T(128)} %constant.13.clone.1), padding=0_1_1x0_0_0x0_0_0 | pad | bytes 1572868 | tf_op jit(solution)/shard_map/pad | solution.py:67
  43.0 0.0 collective-permute-done
  43.0 1.3 maximum_convert_fusion
  44.3 0.1 copy-done.4
  44.3 1.0 slice_add_fusion
  45.4 151.6 %all-gather.2.cloned.1.call-done = bf16[128,16,2048]{2,1,0:T(8,128)(2,1)} async-done(((bf16[1,16,2048]{2,1,0:T(8,128)(2,1)}), bf16[128,16,2048]{2,1,0:T(8,128)(2,1)}) %all-gather.2.cloned.1.call-update) | async-done | bytes 8388624 | tf_op jit(solution)/shard_map/all_gather | solution.py:71
  197.0 7.1 %select_reduce_fusion = f32[16,2048]{1,0:T(8,128)S(1)} fusion(bf16[128,16,2048]{2,1,0:T(8,128)(2,1)} %all-gather.2.cloned.1.call-done, f32[128]{0:T(128)S(1)} %multiply_convert_fusion, f32[16,2048]{1,0:T(8,128)S(1)} %get-tuple-element.13, pred[128]{0:T(512)(128)(4,1)S(1)} %fusion.20), kind=kLoop, calls=%fused_computation.1 | loop fusion | flops 20938752 | bytes 8651392 | tf_op jit(solution)/shard_map/reduce_sum | solution.py:80
  204.0 0.0 copy-done.5
  204.0 0.0 copy-start
  204.1 0.2 multiply_add_fusion
  204.3 1.3 copy-done
  205.6 4.2 %multiply_reduce_fusion = f32[8,16,2048]{2,1,0:T(8,128)S(1)} fusion(f32[8,16,2048]{2,1,0:T(8,128)S(1)} %multiply_add_fusion, f32[16,16,2048]{2,1,0:T(8,128)S(1)} %copy-done), kind=kLoop, calls=%fused_computation | loop fusion | flops 8126464 | bytes 4194304 | tf_op jit(solution)/shard_map/reduce_sum | solution.py:84
  209.8 0.0 copy-start.9
  209.9 0.0 copy-start.10
  209.9 0.1 add.104
  210.0 0.9 copy-done.9
  210.9 0.5 fusion.11
  211.4 0.0 copy-start.1
  211.4 0.2 fusion
  211.6 9.7 %psum.7 = f32[128]{0:T(128)S(1)} all-reduce(f32[128]{0:T(128)S(1)} %fusion), channel_id=1, replica_groups=mesh['seq'=128,'chan'=4] {'chan'}, use_global_device_ids=true, to_apply=%region_6.7 | all-reduce | flops 128 | bytes 1024 | tf_op jit(solution)/shard_map/psum | solution.py:89
  221.3 1.0 fusion.2
  (28 shorter events, 0.3 us)
Async XLA Ops:
  7.2 189.8 %all-gather.2.cloned.1.call-start = ((), (), s32[]{:S(2)}) async-start(), calls=%async_computation | async-start | bytes 8454144 | tf_op jit(solution)/shard_map/all_gather | solution.py:71
  8.0 11.7 %collective-permute-start.1 = (bf16[2,2048]{1,0:T(2,128)(2,1)S(1)}, bf16[2,2048]{1,0:T(2,128)(2,1)S(1)}, u32[]{:S(2)}, u32[]{:S(2)}) collective-permute-start(bf16[2,2048]{1,0:T(2,128)(2,1)S(1)} %slice.156), channel_id=1, source_target_pairs={{0,4},{4,8},{8,12},{12,16},{16,20},{20,24},{24,28},{28,32},{32,36}... | collective-permute-start | bytes 24584 | tf_op jit(solution)/shard_map/ppermute | solution.py:15
  10.7 9.2 %collective-permute-start.2 = (bf16[2,2048]{1,0:T(2,128)(2,1)S(1)}, bf16[2,2048]{1,0:T(2,128)(2,1)S(1)}, u32[]{:S(2)}, u32[]{:S(2)}) collective-permute-start(bf16[2,2048]{1,0:T(2,128)(2,1)S(1)} %slice.163), channel_id=1, source_target_pairs={{0,4},{4,8},{8,12},{12,16},{16,20},{20,24},{24,28},{28,32},{32,36}... | collective-permute-start | bytes 24584 | tf_op jit(solution)/shard_map/ppermute | solution.py:15
  18.7 1.0 copy-start.7
  18.7 1.2 copy-start.8
  26.5 0.9 copy-start.6
  34.9 8.1 %collective-permute-start = (bf16[2,2048]{1,0:T(2,128)(2,1)S(1)}, bf16[2,2048]{1,0:T(2,128)(2,1)S(1)}, u32[]{:S(2)}, u32[]{:S(2)}) collective-permute-start(bf16[2,2048]{1,0:T(2,128)(2,1)S(1)} %slice.149), channel_id=1, source_target_pairs={{0,4},{4,8},{8,12},{12,16},{16,20},{20,24},{24,28},{28,32},{32,36}... | collective-permute-start | bytes 24584 | tf_op jit(solution)/shard_map/ppermute | solution.py:15
  40.5 3.7 %copy-start.3 = (f32[8,16,2048]{2,1,0:T(8,128)S(1)}, f32[8,16,2048]{2,1,0:T(8,128)}, u32[]{:S(2)}) copy-start(f32[8,16,2048]{2,1,0:T(8,128)} %pad.25) | copy-start | bytes 3145732
  43.0 1.4 copy-start.4
  45.4 158.7 %copy-start.5 = (f32[7,16,2048]{2,1,0:T(8,128)S(1)}, f32[7,16,2048]{2,1,0:T(8,128)}, u32[]{:S(2)}) copy-start(f32[7,16,2048]{2,1,0:T(8,128)} %slice_add_fusion) | copy-start | bytes 2752516
  204.0 1.6 copy-start
  205.6 4.2 %copy-start.2 = (f32[8,16,2048]{2,1,0:T(8,128)S(1)}, f32[8,16,2048]{2,1,0:T(8,128)}, u32[]{:S(2)}) copy-start(f32[8,16,2048]{2,1,0:T(8,128)} %get-tuple-element.3) | copy-start | bytes 3145732
  209.8 1.0 copy-start.9
  209.9 1.0 copy-start.10
  210.9 10.4 %copy-start.11 = (f32[2048]{0:T(1024)S(1)}, f32[2048]{0:T(1024)}, u32[]{:S(2)}) copy-start(f32[2048]{0:T(1024)} %param.17) | copy-start | bytes 24580
  211.4 10.9 %copy-start.1 = (bf16[128,2048]{1,0:T(8,128)(2,1)}, bf16[128,2048]{1,0:T(8,128)(2,1)S(1)}, u32[]{:S(2)}) copy-start(bf16[128,2048]{1,0:T(8,128)(2,1)S(1)} %fusion.11) | copy-start | bytes 1572868
Sparse Core Ops, SparseCore 0:
  34.2 162.6 all-gather.1
where the time goes:
time: 230 us; the launch traced here: 229 us
  waiting for transfers between devices  152 us (66%)
  other arithmetic  29.9 us (13%)
  local copies, waits for them, and re-layouts  15.1 us (7%)
  between operations  14.3 us (6%)
  blocking collectives  9.68 us (4%)
  starting transfers between devices  7.56 us (3%)
    all_gather x1, waiting for transfers between devices, body(): lax.all_gather(block_state[None].astype(jnp.bfloat16), 'seq', axis=0, til...  152 us
    psum x1, blocking collectives, body(): row_squares = lax.psum(jnp.sum(widened * widened, axis=1), 'chan')  9.68 us
    ppermute x3, starting transfers between devices, shifted(): return lax.ppermute(block, axis, route)  7.52 us
    reduce_sum x1, other arithmetic, body(): carried = jnp.zeros_like(block_state) + jnp.sum(masked, axis=0)  7.07 us
    pad x4, local copies, waits for them, and re-layouts, body(): lax.associative_scan(link_states, (step_decay, sub_states), axis=0)  6.35 us
    reduce_sum x1, other arithmetic, body(): sub_states = jnp.sum(blocks[:, :, None, :] * tail_decay[None], axis=1)  5.81 us
    unnamed x25, local copies, waits for them, and re-layouts  5.43 us
  transfers between devices with their start and end apart: 4, of which 1 were waited for; matrix products, arithmetic and copies ran while one was open for 7% of the time, Pallas kernels for 0%

commit v1 on v0

--- a/solution.py
+++ b/solution.py
@@ -68,8 +68,11 @@
     block_state = running[sub_count - 1]
     entering = jnp.concatenate([jnp.zeros_like(running[:1]), running[:-1]], axis=0)
     position = lax.axis_index("seq")
-    piece = lax.all_gather(
-        block_state[None].astype(jnp.bfloat16), "seq", axis=0, tiled=True
+    piece = jnp.concatenate(
+        lax.all_to_all(
+            jnp.stack([block_state[None].astype(jnp.bfloat16)] * lax.axis_size("seq")), "seq", 0, 0
+        ),
+        axis=0,
     ).astype(jnp.float32)
     members = piece.shape[0]
     sources = jnp.arange(members, dtype=jnp.int32)

time: 230 us -> 285 us (1.24)
  the two profiles are of different devices: /device:TPU:2 before, /device:TPU:8 now
where the time goes in v1:
time: 285 us; the launch traced here: 284 us
  waiting for transfers between devices  198 us (69%)
  other arithmetic  29.2 us (10%)
  starting transfers between devices  27.6 us (10%)
  local copies, waits for them, and re-layouts  19.3 us (7%)
  blocking collectives  8.37 us (3%)
    ppermute x3, waiting for transfers between devices, shifted(): return lax.ppermute(block, axis, route)  175 us
    all_to_all x1, waiting for transfers between devices, body(): lax.all_to_all(jnp.stack([block_state[None].astype(jnp.bfloat16)] * lax.a...  23.2 us
    all_to_all x1, starting transfers between devices, body(): lax.all_to_all(jnp.stack([block_state[None].astype(jnp.bfloat16)] * lax.a...  20 us
    psum x1, blocking collectives, body(): row_squares = lax.psum(jnp.sum(widened * widened, axis=1), 'chan')  8.37 us
    ppermute x3, starting transfers between devices, shifted(): return lax.ppermute(block, axis, route)  7.63 us
    reduce_sum x1, other arithmetic, body(): carried = jnp.zeros_like(block_state) + jnp.sum(masked, axis=0)  7.08 us
    pad x4, local copies, waits for them, and re-layouts, body(): lax.associative_scan(link_states, (step_decay, sub_states), axis=0)  6.26 us
    reduce_sum x1, other arithmetic, body(): sub_states = jnp.sum(blocks[:, :, None, :] * tail_decay[None], axis=1)  5.83 us
  transfers between devices with their start and end apart: 4, of which 2 were waited for; matrix products, arithmetic and copies ran while one was open for 5% of the time, Pallas kernels for 0%

profile of v1, /device:TPU:8, one launch (start us, length us, event | category | flops | bytes accessed | tf_op | source)
XLA Modules:
  0.0 284.4 jit_solution(1011600190533010923)
XLA Ops:
  0.6 0.8 slice.163
  1.4 1.9 collective-permute-start.2
  3.3 0.8 slice.156
  4.1 3.5 %collective-permute-start.1 = (bf16[2,2048]{1,0:T(2,128)(2,1)S(1)}, bf16[2,2048]{1,0:T(2,128)(2,1)S(1)}, u32[]{:S(2)}, u32[]{:S(2)}) collective-permute-start(bf16[2,2048]{1,0:T(2,128)(2,1)S(1)} %slice.156), channel_id=1, source_target_pairs={{0,4},{4,8},{8,12},{12,16},{16,20},{20,24},{24,28},{28,32},{32,36}... | collective-permute-start | bytes 24584 | tf_op jit(solution)/shard_map/ppermute | solution.py:15
  7.6 1.1 fusion.27
  8.7 1.0 fusion.24
  9.7 2.4 exponential_multiply_fusion
  12.1 1.0 fusion.19
  13.2 0.0 collective-permute-done.2
  13.2 0.0 copy-done.7
  13.2 0.1 maximum_convert_fusion.2
  13.3 0.0 collective-permute-done.1
  13.4 0.1 maximum_convert_fusion.1
  13.5 0.7 fusion.6
  14.2 5.8 %multiply_reduce_fusion.1 = (f32[8,16,2048]{2,1,0:T(8,128)S(1)}, f32[8,16,2048]{2,1,0:T(8,128)}) fusion(f32[16,16,2048]{2,1,0:T(8,128)S(1)} %get-tuple-element.10, f32[8,16,2048]{2,1,0:T(8,128)S(1)} %bitcast.28, f32[16,16,2048]{2,1,0:T(8,128)S(1)} %fusion.19), kind=kLoop, calls=%fused_computation.4 | loop fusion | flops 16252928 | bytes 7340032 | tf_op jit(solution)/shard_map/reduce_sum | solution.py:65
  20.0 0.1 slice_add_fusion.1
  20.1 0.8 copy-done.6
  21.1 0.1 pad.22
  21.1 1.5 pad.23
  22.6 1.1 add.100
  23.7 2.3 pad.62
  26.0 0.9 fusion.21
  26.9 4.3 %stack.2 = bf16[128,1,16,2048]{3,2,1,0:T(8,128)(2,1)} broadcast(bf16[16,2048]{1,0:T(8,128)(2,1)S(1)} %fusion.21), dimensions={2,3} | broadcast | bytes 8454144 | tf_op jit(solution)/shard_map/stack | solution.py:73
  31.2 20.0 %all-to-all-start = ((bf16[128,1,16,2048]{3,2,1,0:T(8,128)(2,1)}), bf16[128,1,16,2048]{3,2,1,0:T(8,128)(2,1)}, u32[]{:S(2)}, u32[]{:S(2)}) async-start(bf16[128,1,16,2048]{3,2,1,0:T(8,128)(2,1)} %stack.2), calls=%async_computation | async-start | bytes 16777216 | tf_op jit(solution)/shard_map/all_to_all | solution.py:72
  51.2 0.8 slice.149
  52.0 2.2 collective-permute-start
  54.2 1.1 fusion.15
  55.4 2.4 pad.25
  57.7 2.3 pad.24
  60.1 174.8 %collective-permute-done = bf16[2,2048]{1,0:T(2,128)(2,1)S(1)} collective-permute-done((bf16[2,2048]{1,0:T(2,128)(2,1)S(1)}, bf16[2,2048]{1,0:T(2,128)(2,1)S(1)}, u32[]{:S(2)}, u32[]{:S(2)}) %collective-permute-start) | collective-permute-done | bytes 8224 | tf_op jit(solution)/shard_map/ppermute | solution.py:15
  234.9 1.2 maximum_convert_fusion
  236.1 1.0 slice_add_fusion
  237.1 23.2 %all-to-all-done = bf16[128,1,16,2048]{3,2,1,0:T(8,128)(2,1)} async-done(((bf16[128,1,16,2048]{3,2,1,0:T(8,128)(2,1)}), bf16[128,1,16,2048]{3,2,1,0:T(8,128)(2,1)}, u32[]{:S(2)}, u32[]{:S(2)}) %all-to-all-start) | async-done | bytes 8388640 | tf_op jit(solution)/shard_map/all_to_all | solution.py:72
  260.3 7.1 %fusion.1 = f32[16,2048]{1,0:T(8,128)S(1)} fusion(bf16[128,1,16,2048]{3,2,1,0:T(8,128)(2,1)} %all-to-all-done, f32[128]{0:T(128)S(1)} %multiply_convert_fusion, f32[16,2048]{1,0:T(8,128)S(1)} %get-tuple-element.13, pred[128]{0:T(512)(128)(4,1)S(1)} %fusion.23), kind=kLoop, calls=%fused_computation.2 | loop fusion | flops 20938752 | bytes 8651392 | tf_op jit(solution)/shard_map/reduce_sum | solution.py:83
  267.4 0.2 multiply_add_fusion
  267.7 1.3 copy-done
  269.0 4.2 %multiply_reduce_fusion = f32[8,16,2048]{2,1,0:T(8,128)S(1)} fusion(f32[8,16,2048]{2,1,0:T(8,128)S(1)} %multiply_add_fusion, f32[16,16,2048]{2,1,0:T(8,128)S(1)} %copy-done), kind=kLoop, calls=%fused_computation.3 | loop fusion | flops 8126464 | bytes 4194304 | tf_op jit(solution)/shard_map/reduce_sum | solution.py:87
  273.2 0.0 copy-start.9
  273.2 0.0 copy-start.10
  273.3 0.1 add.104
  273.4 0.9 copy-done.9
  274.3 0.0 copy-done.10
  274.3 0.5 fusion.13
  274.8 0.0 copy-start.1
  274.8 0.2 fusion.2
  275.0 8.4 %psum.7 = f32[128]{0:T(128)S(1)} all-reduce(f32[128]{0:T(128)S(1)} %fusion.2), channel_id=1, replica_groups=mesh['seq'=128,'chan'=4] {'chan'}, use_global_device_ids=true, to_apply=%region_6.7 | all-reduce | flops 128 | bytes 1024 | tf_op jit(solution)/shard_map/psum | solution.py:92
  283.4 0.0 copy-done.11
  283.4 1.0 fusion.4
  (28 shorter events, 0.3 us)
Async XLA Ops:
  1.4 11.8 %collective-permute-start.2 = (bf16[2,2048]{1,0:T(2,128)(2,1)S(1)}, bf16[2,2048]{1,0:T(2,128)(2,1)S(1)}, u32[]{:S(2)}, u32[]{:S(2)}) collective-permute-start(bf16[2,2048]{1,0:T(2,128)(2,1)S(1)} %slice.163), channel_id=1, source_target_pairs={{0,4},{4,8},{8,12},{12,16},{16,20},{20,24},{24,28},{28,32},{32,36}... | collective-permute-start | bytes 24584 | tf_op jit(solution)/shard_map/ppermute | solution.py:15
  4.1 9.2 %collective-permute-start.1 = (bf16[2,2048]{1,0:T(2,128)(2,1)S(1)}, bf16[2,2048]{1,0:T(2,128)(2,1)S(1)}, u32[]{:S(2)}, u32[]{:S(2)}) collective-permute-start(bf16[2,2048]{1,0:T(2,128)(2,1)S(1)} %slice.156), channel_id=1, source_target_pairs={{0,4},{4,8},{8,12},{12,16},{16,20},{20,24},{24,28},{28,32},{32,36}... | collective-permute-start | bytes 24584 | tf_op jit(solution)/shard_map/ppermute | solution.py:15
  12.1 1.0 copy-start.7
  12.1 1.2 copy-start.8
  20.0 0.9 copy-start.6
  31.2 229.1 %all-to-all-start = ((bf16[128,1,16,2048]{3,2,1,0:T(8,128)(2,1)}), bf16[128,1,16,2048]{3,2,1,0:T(8,128)(2,1)}, u32[]{:S(2)}, u32[]{:S(2)}) async-start(bf16[128,1,16,2048]{3,2,1,0:T(8,128)(2,1)} %stack.2), calls=%async_computation | async-start | bytes 16777216 | tf_op jit(solution)/shard_map/all_to_all | solution.py:72
  52.0 182.9 %collective-permute-start = (bf16[2,2048]{1,0:T(2,128)(2,1)S(1)}, bf16[2,2048]{1,0:T(2,128)(2,1)S(1)}, u32[]{:S(2)}, u32[]{:S(2)}) collective-permute-start(bf16[2,2048]{1,0:T(2,128)(2,1)S(1)} %slice.149), channel_id=1, source_target_pairs={{0,4},{4,8},{8,12},{12,16},{16,20},{20,24},{24,28},{28,32},{32,36}... | collective-permute-start | bytes 24584 | tf_op jit(solution)/shard_map/ppermute | solution.py:15
  57.7 178.3 %copy-start.3 = (f32[8,16,2048]{2,1,0:T(8,128)S(1)}, f32[8,16,2048]{2,1,0:T(8,128)}, u32[]{:S(2)}) copy-start(f32[8,16,2048]{2,1,0:T(8,128)} %pad.25) | copy-start | bytes 3145732
  60.1 176.0 %copy-start.4 = (f32[8,16,2048]{2,1,0:T(8,128)S(1)}, f32[8,16,2048]{2,1,0:T(8,128)}, u32[]{:S(2)}) copy-start(f32[8,16,2048]{2,1,0:T(8,128)} %pad.24) | copy-start | bytes 3145732
  237.1 30.3 %copy-start.5 = (f32[7,16,2048]{2,1,0:T(8,128)S(1)}, f32[7,16,2048]{2,1,0:T(8,128)}, u32[]{:S(2)}) copy-start(f32[7,16,2048]{2,1,0:T(8,128)} %slice_add_fusion) | copy-start | bytes 2752516
  267.4 1.6 copy-start
  269.0 4.2 %copy-start.2 = (f32[8,16,2048]{2,1,0:T(8,128)S(1)}, f32[8,16,2048]{2,1,0:T(8,128)}, u32[]{:S(2)}) copy-start(f32[8,16,2048]{2,1,0:T(8,128)} %get-tuple-element.3) | copy-start | bytes 3145732
  273.2 1.0 copy-start.9
  273.2 1.0 copy-start.10
  274.3 9.1 %copy-start.11 = (f32[2048]{0:T(1024)S(1)}, f32[2048]{0:T(1024)}, u32[]{:S(2)}) copy-start(f32[2048]{0:T(1024)} %param.17) | copy-start | bytes 24580
  274.8 9.6 %copy-start.1 = (bf16[128,2048]{1,0:T(8,128)(2,1)}, bf16[128,2048]{1,0:T(8,128)(2,1)S(1)}, u32[]{:S(2)}) copy-start(bf16[128,2048]{1,0:T(8,128)(2,1)S(1)} %fusion.13) | copy-start | bytes 1572868
